TPU v7x, 256 devices: a whole 4x4x8 slice. The times are simulated.
256 devices in a mesh: seq: 64 (over y, z, core), head: 4 (over x).
Axes of the slice: x: 4, y: 4, z: 8, core: 2. Of those that a mesh axis runs over, the one named last changes fastest.
Arguments:
- queries: bfloat16 [12288, 4096], P('seq', 'head'), may hold values from -125 to 125
- key_vectors: bfloat16 [12288, 4096], P('seq', 'head'), may hold values from -21 to 21
- values: bfloat16 [12288, 4096], P('seq', 'head'), may hold values from -6 to 6
- cotangent: bfloat16 [12288, 4096], P('seq', 'head'), may hold values from -6 to 6
- cluster: int32 [12288, 1], P('seq'), may hold values from 0 to 15; in each aligned block of 192 rows (0 to 191, 192 to 383, ...) at most 24 rows name the same one
- block_pattern: int32 [16, 96, 96], replicated, may hold values from 0 to 1, as said below
Outputs:
- attended: bfloat16 [12288, 4096], P('seq', 'head')
- query_grad: bfloat16 [12288, 4096], P('seq', 'head')
- key_grad: bfloat16 [12288, 4096], P('seq', 'head')
- value_grad: bfloat16 [12288, 4096], P('seq', 'head')
Inputs may be any that keep to these rules, and one draw needn't show every extreme that they name: Within the rows of one device no cluster is named by more than 24 rows, and in every draw some cluster is named by exactly 24 rows of some device. Every diagonal entry block_pattern[g, b, b] is 1.
All inputs are finite; a program needn't handle non-finite values.
Results may differ from a plain program's by a relative error of at most 0.0061.
Values may be sent and summed in bfloat16 or wider, within the bound.
A program may use at most 128 MiB of HBM per device.

v0:
```python
import jax
import jax.numpy as jnp
from jax import lax
from jax.sharding import PartitionSpec as P

HEADS = 32
HEAD_DIM = 128
GS = 4
BLK = 128
NEG_FILL = -1e30
EPSILON = 1e-05


def from_partner(value, axis, bit):
    mask = 2**bit
    pairs = [(source, source ^ mask) for source in range(lax.axis_size(axis))]
    return lax.ppermute(value, axis, pairs)


def contract_last(left_side, right_side):
    return lax.dot_general(
        left_side, right_side, (((1,), (1,)), ((), ())), preferred_element_type=jnp.float32
    )


def contract_first(left_side, right_side):
    return lax.dot_general(
        left_side, right_side, (((0,), (0,)), ((), ())), preferred_element_type=jnp.float32
    )


def visible_mask(pattern, query_pos, query_live, key_pos, key_live):
    pattern_rows = pattern[query_pos // BLK]
    allowed = jnp.take(pattern_rows, key_pos // BLK, axis=1) == 1
    causal = key_pos[None, :] <= query_pos[:, None]
    return allowed & causal & query_live[:, None] & key_live[None, :]


def cluster_ranks(table, cluster_index):
    source_count, tok_count = table.shape
    in_cluster = table == cluster_index
    token_iota = jnp.arange(tok_count, dtype=jnp.int32)
    earlier_table = (token_iota[:, None] < token_iota[None, :]).astype(jnp.bfloat16)
    earlier = jnp.dot(
        in_cluster.astype(jnp.bfloat16), earlier_table, preferred_element_type=jnp.float32
    ).astype(jnp.int32)
    global_pos = (
        jnp.arange(source_count, dtype=jnp.int32)[:, None] * tok_count + token_iota[None, :]
    )
    return (in_cluster, earlier, global_pos)


def code_positions(slot_code, global_pos, capacity):
    matches = slot_code[:, :, None] == jnp.arange(capacity, dtype=jnp.int32)[None, None, :]
    positions = jnp.sum(jnp.where(matches, global_pos[:, :, None], 0), axis=1)
    occupied = jnp.any(matches, axis=1)
    return (positions, occupied)


def slot_positions(table, cluster_index, slot_count):
    source_count = table.shape[0]
    capacity = GS * slot_count
    in_cluster, earlier, global_pos = cluster_ranks(table, cluster_index)
    slot_code = jnp.where(in_cluster, earlier % GS * slot_count + earlier // GS, -1)
    positions, occupied = code_positions(slot_code, global_pos, capacity)
    positions = (
        positions.reshape(source_count, GS, slot_count)
        .transpose(1, 0, 2)
        .reshape(GS, source_count * slot_count)
    )
    occupied = (
        occupied.reshape(source_count, GS, slot_count)
        .transpose(1, 0, 2)
        .reshape(GS, source_count * slot_count)
    )
    return (positions, occupied)


def swap_keys(piece_now, bit_index):
    return from_partner(piece_now, "seq", bit_index)


def swap_grads(piece_now, bit_index):
    return from_partner(piece_now, "seq", bit_index)


def dispatch_rows(outgoing):
    return lax.all_to_all(outgoing, "seq", split_axis=1, concat_axis=1, tiled=True)


def combine_rows(outgoing):
    return lax.all_to_all(outgoing, "seq", split_axis=1, concat_axis=1, tiled=True)


def collect(local_piece, member, along, swapper):
    combined = local_piece
    for bit_index in range(GS.bit_length() - 1):
        partner_piece = swapper(combined, bit_index)
        lower_side = member // 2**bit_index % 2 == 0
        combined = jnp.where(
            lower_side,
            jnp.concatenate([combined, partner_piece], along),
            jnp.concatenate([partner_piece, combined], along),
        )
    return combined


def reduce_to_member(all_terms, member, swapper):
    current = all_terms
    for bit_index in reversed(range(GS.bit_length() - 1)):
        half_rows = current.shape[1] // 2
        lower_side = member // 2**bit_index % 2 == 0
        low_half = current[:, :half_rows]
        high_half = current[:, half_rows:]
        kept = jnp.where(lower_side, low_half, high_half)
        given = jnp.where(lower_side, high_half, low_half)
        current = kept + swapper(given, bit_index)
    return current


def forward_heads(query_slots, key_slots, value_slots, grad_slots, visible, score_scale):
    query_count, features = query_slots.shape
    key_count = key_slots.shape[0]
    head_count = features // HEAD_DIM
    attended = jnp.zeros((query_count, features), jnp.bfloat16)
    query_grad = jnp.zeros((query_count, features), jnp.bfloat16)
    side_result = jnp.zeros((2, key_count, features), jnp.float32)

    def one_head(head_index, running):
        attended_acc, query_acc, side_acc = running
        column_start = head_index * HEAD_DIM
        query_rows = lax.dynamic_slice_in_dim(query_slots, column_start, HEAD_DIM, 1)
        key_rows = lax.dynamic_slice_in_dim(key_slots, column_start, HEAD_DIM, 1)
        value_rows = lax.dynamic_slice_in_dim(value_slots, column_start, HEAD_DIM, 1)
        grad_rows = lax.dynamic_slice_in_dim(grad_slots, column_start, HEAD_DIM, 1)
        scores = jnp.where(visible, contract_last(query_rows, key_rows) * score_scale, NEG_FILL)
        row_max = jnp.max(scores, axis=1, keepdims=True)
        weights = jnp.where(visible, jnp.exp(scores - row_max), 0.0)
        row_total = jnp.maximum(jnp.sum(weights, axis=1, keepdims=True), 1.0)
        probabilities = weights / row_total
        prob_half = probabilities.astype(jnp.bfloat16)
        attended_head = jnp.dot(prob_half, value_rows, preferred_element_type=jnp.float32).astype(
            jnp.bfloat16
        )
        prob_grad = contract_last(grad_rows, value_rows)
        row_delta = jnp.sum(probabilities * prob_grad, axis=1, keepdims=True)
        score_grad = (probabilities * (prob_grad - row_delta)).astype(jnp.bfloat16)
        query_head = (
            jnp.dot(score_grad, key_rows, preferred_element_type=jnp.float32) * score_scale
        ).astype(jnp.bfloat16)
        attended_acc = lax.dynamic_update_slice_in_dim(attended_acc, attended_head, column_start, 1)
        query_acc = lax.dynamic_update_slice_in_dim(query_acc, query_head, column_start, 1)
        key_part = contract_first(score_grad, query_rows)
        value_part = contract_first(prob_half, grad_rows)
        side_acc = lax.dynamic_update_slice_in_dim(
            side_acc, jnp.stack([key_part, value_part]), column_start, 2
        )
        return (attended_acc, query_acc, side_acc)

    return lax.fori_loop(0, head_count, one_head, (attended, query_grad, side_result))


def per_device(queries, key_vectors, values, cotangent, cluster, block_pattern):
    seq_count = lax.axis_size("seq")
    tok_count, features = queries.shape
    slot_count = 2 * tok_count // seq_count
    received = seq_count * slot_count
    group_count = seq_count // GS
    score_scale = HEAD_DIM ** (-0.5)
    my_index = lax.axis_index("seq")
    group_index = my_index // GS
    member = my_index % GS
    key_float = key_vectors.astype(jnp.float32)
    square_sum = lax.psum(jnp.sum(key_float * key_float, axis=1), "head")
    key_rms = jnp.sqrt(square_sum / (HEADS * HEAD_DIM) + EPSILON)[:, None]
    normed_float = key_float / key_rms
    normed = normed_float.astype(jnp.bfloat16)
    own_ids = cluster[:, 0]
    everyone = lax.all_gather(own_ids, "seq", axis=0, tiled=True)
    table = everyone.reshape(seq_count, tok_count)
    token_iota = jnp.arange(tok_count, dtype=jnp.int32)
    onehot_own = (own_ids[:, None] == jnp.arange(group_count, dtype=jnp.int32)[None, :]).astype(
        jnp.bfloat16
    )
    before_table = (token_iota[:, None] > token_iota[None, :]).astype(jnp.bfloat16)
    before = jnp.dot(before_table, onehot_own, preferred_element_type=jnp.float32)
    own_rank = jnp.sum(before * onehot_own.astype(jnp.float32), axis=1).astype(jnp.int32)
    pattern = lax.dynamic_index_in_dim(block_pattern, group_index, 0, keepdims=False)
    stacked_inputs = jnp.stack([queries, normed, values, cotangent])
    destination = own_ids * GS + own_rank % GS
    send_slot = destination * slot_count + own_rank // GS
    outgoing = jnp.zeros((4, received, features), jnp.bfloat16).at[:, send_slot].set(stacked_inputs)
    arrived = dispatch_rows(outgoing)
    key_positions, key_present = slot_positions(table, group_index, slot_count)
    query_positions = lax.dynamic_index_in_dim(key_positions, member, 0, keepdims=False)
    query_present = lax.dynamic_index_in_dim(key_present, member, 0, keepdims=False)
    flat_positions = key_positions.reshape(-1)
    flat_present = key_present.reshape(-1)
    visible = visible_mask(pattern, query_positions, query_present, flat_positions, flat_present)
    key_value = collect(arrived[1:3], member, 1, swap_keys)
    attended, query_grad, both_terms = forward_heads(
        arrived[0], key_value[0], key_value[1], arrived[3], visible, score_scale
    )
    reduced = reduce_to_member(both_terms, member, swap_grads)
    key_part = reduced[0]
    value_part = reduced[1]
    normed_grad = (key_part * score_scale).astype(jnp.bfloat16)
    value_slots = value_part.astype(jnp.bfloat16)
    outgoing_back = jnp.stack([attended, query_grad, normed_grad, value_slots])
    returned = combine_rows(outgoing_back)
    home_rows = returned[:, send_slot]
    grad_float = home_rows[2].astype(jnp.float32)
    inner = lax.psum(jnp.sum(normed_float * grad_float, axis=1), "head")
    key_grad = (
        (grad_float - normed_float * (inner / (HEADS * HEAD_DIM))[:, None]) / key_rms
    ).astype(jnp.bfloat16)
    return (home_rows[0], home_rows[1], key_grad, home_rows[3])


def solution(mesh):
    in_specs = (
        P("seq", "head"),
        P("seq", "head"),
        P("seq", "head"),
        P("seq", "head"),
        P("seq", None),
        P(),
    )
    out_specs = (P("seq", "head"), P("seq", "head"), P("seq", "head"), P("seq", "head"))
    return jax.shard_map(
        per_device, mesh=mesh, in_specs=in_specs, out_specs=out_specs, check_vma=False
    )
```

profile of v0, /device:TPU:2, one launch (start us, length us, event | category | flops | bytes accessed | tf_op | source)
XLA Modules:
  0.0 935.9 jit_solution(13777769954462944271)
XLA Ops:
  3.5 10.0 %psum.14 = f32[192]{0:T(256)S(1)} all-reduce(f32[192]{0:T(256)S(1)} %fusion.30), channel_id=1, replica_groups=mesh['seq'=64,'head'=4] {'head'}, use_global_device_ids=true, to_apply=%region_2.3 | all-reduce | flops 192 | bytes 1536 | tf_op jit(solution)/shard_map/psum | solution.py:174
  17.2 2.5 broadcast_in_dim.72
  19.7 22.8 %scatter_fusion = bf16[4,384,1024]{2,0,1:T(4,128)(2,1)} fusion(bf16[4,384,1024]{2,0,1:T(4,128)(2,1)} %broadcast_in_dim.72, s32[192]{0:T(256)S(1)} %bitcast.92, bf16[192,4,1024]{2,1,0:T(4,128)(2,1)S(1)} %copy.35), kind=kCustom, calls=%fused_computation.3 | custom fusion | bytes 4719360 | tf_op jit(solution)/shard_map/scatter | solution.py:192
  42.5 83.7 %all_to_all.10 = bf16[4,384,1024]{2,0,1:T(4,128)(2,1)S(1)} all-to-all(bf16[4,384,1024]{2,0,1:T(4,128)(2,1)} %scatter_fusion), channel_id=1, replica_groups=mesh['seq'=64,'head'=4] {'seq'}, dimensions={1} | all-to-all | bytes 6291456 | tf_op jit(solution)/shard_map/all_to_all | solution.py:88
  126.2 1.7 copy-done.2
  127.9 1.8 slice.68
  131.8 248.5 %all-reduce = s32[12288]{0:T(1024)S(1)} all-reduce(s32[12288]{0:T(1024)S(1)} %dynamic-update-slice), channel_id=2, replica_groups=mesh['seq'=64,'head'=4] {'seq'}, use_global_device_ids=true, to_apply=%add | all-reduce | flops 12288 | bytes 98304
  380.4 16.6 %broadcast_select_fusion.2 = bf16[2,768,1024]{2,0,1:T(2,128)(2,1)} fusion(pred[]{:T(512)S(6)} %eq.66, bf16[2,384,1024]{2,0,1:T(2,128)(2,1)} %collective-permute-done, bf16[2,384,1024]{2,0,1:T(2,128)(2,1)S(1)} %slice.68), kind=kLoop, calls=%fused_computation.41 | loop fusion | flops 4718592 | bytes 6291457 | tf_op jit(solution)/shard_map/jit(_where)/select_n | solution.py:100
  402.7 3.7 gather_fusion.1
  406.5 1.5 fusion.26
  408.7 2.2 fusion.52
  412.4 49.9 %collective-permute-done.1 = bf16[2,768,1024]{2,0,1:T(2,128)(2,1)} collective-permute-done((bf16[2,768,1024]{2,0,1:T(2,128)(2,1)}, bf16[2,768,1024]{2,0,1:T(2,128)(2,1)}, u32[]{:S(2)}, u32[]{:S(2)}) %collective-permute-start.1) | collective-permute-done | bytes 3145760 | tf_op jit(solution)/shard_map/ppermute | solution.py:17
  462.4 30.7 %broadcast_select_fusion = bf16[2,1536,1024]{2,0,1:T(2,128)(2,1)S(1)} fusion(pred[]{:T(512)S(6)} %eq.65, bf16[2,768,1024]{2,0,1:T(2,128)(2,1)} %collective-permute-done.1, bf16[2,768,1024]{2,0,1:T(2,128)(2,1)} %broadcast_select_fusion.2), kind=kLoop, calls=%fused_computation.38 | loop fusion | flops 9437184 | bytes 12582913 | tf_op jit(solution)/shard_map/jit(_where)/select_n | solution.py:100
  493.1 9.8 %fusion.51 = (bf16[1,1536,1024]{2,0,1:T(2,128)(2,1)S(1)}, bf16[1,1536,1024]{2,0,1:T(2,128)(2,1)}) fusion(bf16[2,1536,1024]{2,0,1:T(2,128)(2,1)S(1)} %broadcast_select_fusion), kind=kLoop, calls=%fused_computation.137 | loop fusion | bytes 12582912 | tf_op jit(solution)/shard_map/slice | solution.py:202
  502.9 8.0 copy_bitcast_fusion
  511.1 4.9 broadcast_in_dim.71.clone
  516.0 143.0 %while.17 = (s32[]{:T(128)}, bf16[384,1024]{1,0:T(8,128)(2,1)S(1)}, bf16[384,1024]{1,0:T(8,128)(2,1)S(1)}, f32[2,1536,1024]{2,0,1:T(2,128)}, bf16[384,1024]{1,0:...) while((s32[]{:T(128)}, bf16[384,1024]{1,0:T(8,128)(2,1)S(1)}, ...), condition=%wide.region_10.11_spmd, body=%wide.region_6.10_spmd.sunk | while | flops 915946752 | bytes 36587200 | solution.py:160
  527.4 1.7 fusion.77
  529.8 2.0 multiply_reduce_fusion.2
  533.6 1.5 fusion.80
  537.2 6.7 copy_dynamic-update-slice_fusion.2
  543.9 1.6 fusion.77
  546.2 2.0 multiply_reduce_fusion.2
  550.1 1.5 fusion.80
  553.6 6.7 copy_dynamic-update-slice_fusion.2
  560.4 1.7 fusion.77
  562.7 2.0 multiply_reduce_fusion.2
  566.5 1.5 fusion.80
  570.1 6.7 copy_dynamic-update-slice_fusion.2
  576.8 1.7 fusion.77
  579.2 2.0 multiply_reduce_fusion.2
  583.0 1.5 fusion.80
  586.6 6.7 copy_dynamic-update-slice_fusion.2
  593.3 1.7 fusion.77
  595.7 2.0 multiply_reduce_fusion.2
  597.7 1.5 fusion.79
  599.5 1.5 fusion.80
  603.1 6.7 copy_dynamic-update-slice_fusion.2
  609.7 1.7 fusion.77
  612.1 2.0 multiply_reduce_fusion.2
  615.9 1.5 fusion.80
  619.5 6.7 copy_dynamic-update-slice_fusion.2
  626.1 1.7 fusion.77
  628.5 2.0 multiply_reduce_fusion.2
  632.3 1.5 fusion.80
  635.9 6.7 copy_dynamic-update-slice_fusion.2
  642.6 1.7 fusion.77
  645.0 2.0 multiply_reduce_fusion.2
  648.8 1.5 fusion.80
  652.4 6.7 copy_dynamic-update-slice_fusion.2
  659.0 10.5 %broadcast_select_fusion.1 = f32[2,768,1024]{2,0,1:T(2,128)} fusion(pred[]{:T(512)S(6)} %eq.65, f32[2,1536,1024]{2,0,1:T(2,128)} %get-tuple-element.162), kind=kLoop, calls=%fused_computation.40 | loop fusion | flops 1572864 | bytes 18874368 | tf_op jit(solution)/shard_map/jit(_where)/select_n | solution.py:116
  669.7 131.3 %collective-permute-done.2 = f32[2,768,1024]{2,0,1:T(2,128)S(1)} collective-permute-done((f32[2,768,1024]{2,0,1:T(2,128)}, f32[2,768,1024]{2,0,1:T(2,128)S(1)}, u32[]{:S(2)}, u32[]{:S(2)}) %collective-permute-start.2) | collective-permute-done | bytes 6291488 | tf_op jit(solution)/shard_map/ppermute | solution.py:17
  801.1 10.0 %select_add_fusion = f32[2,768,1024]{2,0,1:T(2,128)S(1)} fusion(f32[2,768,1024]{2,0,1:T(2,128)S(1)} %collective-permute-done.2, pred[]{:T(512)S(6)} %eq.65, f32[2,1536,1024]{2,0,1:T(2,128)} %get-tuple-element.162), kind=kLoop, calls=%fused_computation.39 | loop fusion | flops 3145728 | bytes 25165824 | tf_op jit(solution)/shard_map/add | solution.py:117
  811.1 1.6 broadcast_select_fusion.3
  815.3 3.2 collective-permute-done.3
  818.5 2.7 select_add_fusion.1
  821.1 1.6 slice.93
  822.8 1.6 fusion.27
  824.4 8.4 pad_maximum_fusion.1
  832.8 9.0 all-to-all-start.1
  841.8 72.7 %all-to-all-done.1 = bf16[4,384,1024]{2,0,1:T(4,128)(2,1)} async-done(((bf16[4,384,1024]{2,0,1:T(4,128)(2,1)}), bf16[4,384,1024]{2,0,1:T(4,128)(2,1)}, u32[]{:S(2)}, u32[]{:S(2)}) %all-to-all-start.1) | async-done | bytes 3145760 | tf_op jit(solution)/shard_map/all_to_all | solution.py:92
  914.5 3.8 gather_fusion.2
  918.4 3.0 fusion.53
  923.5 10.1 %psum.15 = f32[192]{0:T(256)S(1)} all-reduce(f32[192]{0:T(256)S(1)} %fusion.31), channel_id=1, replica_groups=mesh['seq'=64,'head'=4] {'head'}, use_global_device_ids=true, to_apply=%region_12.13 | all-reduce | flops 192 | bytes 1536 | tf_op jit(solution)/shard_map/psum | solution.py:213
  (127 shorter events, 57.5 us)
Async XLA Ops:
  0.6 400.7 %copy-start = (s32[16,96,96]{2,1,0:T(8,128)S(1)}, s32[16,96,96]{2,1,0:T(8,128)}, u32[]{:S(2)}) copy-start(s32[16,96,96]{2,1,0:T(8,128)} %param.13) | copy-start | bytes 1769476
  126.2 1.7 copy-start.2
  127.9 2.4 copy-start.7
  127.9 3.6 copy-start.6
  129.7 250.7 %collective-permute-start = (bf16[2,384,1024]{2,0,1:T(2,128)(2,1)S(1)}, bf16[2,384,1024]{2,0,1:T(2,128)(2,1)}, u32[]{:S(2)}, u32[]{:S(2)}) collective-permute-start(bf16[2,384,1024]{2,0,1:T(2,128)(2,1)S(1)} %slice.68), channel_id=1, source_target_pairs={{0,4},{4,0},{8,12},{12,8},{16,20},{20,16},{24,28},{28,24},{32,36},... | collective-permute-start | bytes 4718600 | tf_op jit(solution)/shard_map/ppermute | solution.py:17
  397.0 65.4 %collective-permute-start.1 = (bf16[2,768,1024]{2,0,1:T(2,128)(2,1)}, bf16[2,768,1024]{2,0,1:T(2,128)(2,1)}, u32[]{:S(2)}, u32[]{:S(2)}) collective-permute-start(bf16[2,768,1024]{2,0,1:T(2,128)(2,1)} %broadcast_select_fusion.2), channel_id=1, source_target_pairs={{0,8},{4,12},{8,0},{12,4},{16,24},{20,28},{24,16},{28,20},{32,40},... | collective-permute-start | bytes 9437192 | tf_op jit(solution)/shard_map/ppermute | solution.py:17
  406.4 2.3 copy-start.3
  669.5 131.6 %collective-permute-start.2 = (f32[2,768,1024]{2,0,1:T(2,128)}, f32[2,768,1024]{2,0,1:T(2,128)S(1)}, u32[]{:S(2)}, u32[]{:S(2)}) collective-permute-start(f32[2,768,1024]{2,0,1:T(2,128)} %broadcast_select_fusion.1), channel_id=1, source_target_pairs={{0,8},{4,12},{8,0},{12,4},{16,24},{20,28},{24,16},{28,20},{32,40},... | collective-permute-start | bytes 18874376 | tf_op jit(solution)/shard_map/ppermute | solution.py:17
  812.7 5.7 collective-permute-start.3
  832.8 81.8 %all-to-all-start.1 = ((bf16[4,384,1024]{2,0,1:T(4,128)(2,1)}), bf16[4,384,1024]{2,0,1:T(4,128)(2,1)}, u32[]{:S(2)}, u32[]{:S(2)}) async-start(bf16[4,384,1024]{2,0,1:T(4,128)(2,1)} %pad_maximum_fusion.1), calls=%async_computation.1 | async-start | bytes 6291456 | tf_op jit(solution)/shard_map/all_to_all | solution.py:92
  921.4 1.7 copy-start.4
  921.4 13.3 %copy-start.5 = (bf16[1,192,1024]{2,0,1:T(2,128)(2,1)S(1)}, bf16[1,192,1024]{2,0,1:T(2,128)(2,1)}, u32[]{:S(2)}) copy-start(bf16[1,192,1024]{2,0,1:T(2,128)(2,1)} %get-tuple-element.226) | copy-start | bytes 1179652
  922.3 13.3 %copy-start.1 = (s32[16,96,96]{2,1,0:T(8,128)S(1)}, s32[16,96,96]{2,1,0:T(8,128)}, u32[]{:S(2)}) copy-start(s32[16,96,96]{2,1,0:T(8,128)} %param.13) | copy-start | bytes 1769476
where the time goes:
time: 946 us; the launch traced here: 936 us
  blocking collectives  352 us (37%)
  waiting for transfers between devices  257 us (27%)
  local copies, waits for them, and re-layouts  128 us (14%)
  other arithmetic  104 us (11%)
  matrix products  70.3 us (7%)
  loops' own time  11.8 us (1%)
  starting transfers between devices  10.3 us (1%)
    unnamed x1, blocking collectives  249 us
    ppermute x4, waiting for transfers between devices, from_partner(): return lax.ppermute(value, axis, pairs)  184 us
    all_to_all x1, blocking collectives, dispatch_rows(): lax.all_to_all(outgoing, 'seq', split_axis=1, concat_axis=1, tiled=True)  83.7 us
    all_to_all x1, waiting for transfers between devices, combine_rows(): lax.all_to_all(outgoing, 'seq', split_axis=1, concat_axis=1, tiled=True)  72.7 us
    dynamic_update_slice x8, local copies, waits for them, and re-layouts, one_head(): lax.dynamic_update_slice_in_dim(side_acc, jnp.stack([key_part, value_part...  53.5 us
    select_n x2, other arithmetic, collect(): jnp.where(lower_side, jnp.concatenate([combined, partner_piece], along),...  47.3 us
    dot_general x16, matrix products, contract_last(): lax.dot_general(left_side, right_side, (((1,), (1,)), ((), ())), preferre...  29.5 us
    scatter x1, local copies, waits for them, and re-layouts, per_device(): jnp.zeros((4, received, features), jnp.bfloat16).at[:, send_slot]  22.8 us
  transfers between devices with their start and end apart: 5, of which 4 were waited for; matrix products, arithmetic and copies ran while one was open for 2% of the time, Pallas kernels for 0%

commit v1 on v0

--- a/solution.py
+++ b/solution.py
@@ -89,7 +89,10 @@
 
 
 def combine_rows(outgoing):
-    return lax.all_to_all(outgoing, "seq", split_axis=1, concat_axis=1, tiled=True)
+    return jnp.concatenate(
+        lax.all_to_all(jnp.stack(jnp.split(outgoing, lax.axis_size("seq"), axis=1)), "seq", 0, 0),
+        axis=1,
+    )
 
 
 def collect(local_piece, member, along, swapper):

time: 946 us -> 900 us (0.951)
  local copies, waits for them, and re-layouts: 128 us -> 81.4 us
  loops' own time: 11.8 us -> 0.49 us
  starting transfers between devices: 10.3 us -> 19.9 us
    dynamic_update_slice x8 -> x0, local copies, waits for them, and re-layouts: 53.5 us -> none  [one_head(): lax.dynamic_update_slice_in_dim(side_acc, jnp.stack([key_part, value_part...]
    another operation x1, loops' own time: 11.8 us -> 0.49 us  [forward_heads(): lax.fori_loop(0, head_count, one_head, (attended, query_grad, side_result))]
    dynamic_update_slice x0 -> x8, other arithmetic: none -> 10.9 us  [one_head(): lax.dynamic_update_slice_in_dim(side_acc, jnp.stack([key_part, value_part...]
where the time goes in v1:
time: 900 us; the launch traced here: 890 us
  blocking collectives  352 us (39%)
  waiting for transfers between devices  260 us (29%)
  other arithmetic  103 us (11%)
  local copies, waits for them, and re-layouts  81.4 us (9%)
  matrix products  70.3 us (8%)
  starting transfers between devices  19.9 us (2%)
    unnamed x1, blocking collectives  249 us
    ppermute x4, waiting for transfers between devices, from_partner(): return lax.ppermute(value, axis, pairs)  187 us
    all_to_all x1, blocking collectives, dispatch_rows(): lax.all_to_all(outgoing, 'seq', split_axis=1, concat_axis=1, tiled=True)  83.8 us
    all_to_all x1, waiting for transfers between devices, combine_rows(): lax.all_to_all(jnp.stack(jnp.split(outgoing, lax.axis_size('seq'), axis=1...  72.7 us
    select_n x2, other arithmetic, collect(): jnp.where(lower_side, jnp.concatenate([combined, partner_piece], along),...  47.3 us
    dot_general x16, matrix products, contract_last(): lax.dot_general(left_side, right_side, (((1,), (1,)), ((), ())), preferre...  29.5 us
    scatter x1, local copies, waits for them, and re-layouts, per_device(): jnp.zeros((4, received, features), jnp.bfloat16).at[:, send_slot]  22.8 us
  transfers between devices with their start and end apart: 5, of which 4 were waited for; matrix products, arithmetic and copies ran while one was open for 2% of the time, Pallas kernels for 0%

profile of v1, /device:TPU:2, one launch (start us, length us, event | category | flops | bytes accessed | tf_op | source)
XLA Modules:
  0.0 889.5 jit_solution(11847647258435794512)
XLA Ops:
  3.5 10.0 %psum.14 = f32[192]{0:T(256)S(1)} all-reduce(f32[192]{0:T(256)S(1)} %fusion.30), channel_id=1, replica_groups=mesh['seq'=64,'head'=4] {'head'}, use_global_device_ids=true, to_apply=%region_2.3 | all-reduce | flops 192 | bytes 1536 | tf_op jit(solution)/shard_map/psum | solution.py:177
  14.6 1.4 maximum_bitcast_fusion
  17.2 2.5 broadcast_in_dim.72
  19.7 22.8 %scatter_fusion = bf16[4,384,1024]{2,0,1:T(4,128)(2,1)} fusion(bf16[4,384,1024]{2,0,1:T(4,128)(2,1)} %broadcast_in_dim.72, s32[192]{0:T(256)S(1)} %bitcast.351, bf16[192,4,1024]{2,1,0:T(4,128)(2,1)S(1)} %copy.50), kind=kCustom, calls=%fused_computation.3 | custom fusion | bytes 4719360 | tf_op jit(solution)/shard_map/scatter | solution.py:195
  42.5 83.8 %all_to_all.10 = bf16[4,384,1024]{2,0,1:T(4,128)(2,1)S(1)} all-to-all(bf16[4,384,1024]{2,0,1:T(4,128)(2,1)} %scatter_fusion), channel_id=1, replica_groups=mesh['seq'=64,'head'=4] {'seq'}, dimensions={1} | all-to-all | bytes 6291456 | tf_op jit(solution)/shard_map/all_to_all | solution.py:88
  126.4 1.7 copy-done.3
  128.0 1.8 slice.68
  132.0 248.5 %all-reduce = s32[12288]{0:T(1024)S(1)} all-reduce(s32[12288]{0:T(1024)S(1)} %dynamic-update-slice), channel_id=2, replica_groups=mesh['seq'=64,'head'=4] {'seq'}, use_global_device_ids=true, to_apply=%add | all-reduce | flops 12288 | bytes 98304
  380.5 16.6 %broadcast_select_fusion.1 = bf16[2,768,1024]{2,0,1:T(2,128)(2,1)} fusion(pred[]{:T(512)S(6)} %eq.66, bf16[2,384,1024]{2,0,1:T(2,128)(2,1)} %collective-permute-done, bf16[2,384,1024]{2,0,1:T(2,128)(2,1)S(1)} %slice.68), kind=kLoop, calls=%fused_computation.39 | loop fusion | flops 4718592 | bytes 6291457 | tf_op jit(solution)/shard_map/jit(_where)/select_n | solution.py:103
  397.1 9.6 %collective-permute-start.1 = (bf16[2,768,1024]{2,0,1:T(2,128)(2,1)}, bf16[2,768,1024]{2,0,1:T(2,128)(2,1)}, u32[]{:S(2)}, u32[]{:S(2)}) collective-permute-start(bf16[2,768,1024]{2,0,1:T(2,128)(2,1)} %broadcast_select_fusion.1), channel_id=1, source_target_pairs={{0,8},{4,12},{8,0},{12,4},{16,24},{20,28},{24,16},{28,20},{32,40},... | collective-permute-start | bytes 9437192 | tf_op jit(solution)/shard_map/ppermute | solution.py:17
  412.1 3.7 gather_fusion.1
  415.9 1.5 fusion.26
  418.2 2.2 fusion.52
  420.4 1.5 copy_bitcast_fusion.2
  421.9 49.9 %collective-permute-done.1 = bf16[2,768,1024]{2,0,1:T(2,128)(2,1)} collective-permute-done((bf16[2,768,1024]{2,0,1:T(2,128)(2,1)}, bf16[2,768,1024]{2,0,1:T(2,128)(2,1)}, u32[]{:S(2)}, u32[]{:S(2)}) %collective-permute-start.1) | collective-permute-done | bytes 3145760 | tf_op jit(solution)/shard_map/ppermute | solution.py:17
  471.8 30.7 %broadcast_select_fusion = bf16[2,1536,1024]{2,0,1:T(2,128)(2,1)S(1)} fusion(pred[]{:T(512)S(6)} %eq.65, bf16[2,768,1024]{2,0,1:T(2,128)(2,1)} %collective-permute-done.1, bf16[2,768,1024]{2,0,1:T(2,128)(2,1)} %broadcast_select_fusion.1), kind=kLoop, calls=%fused_computation.37 | loop fusion | flops 9437184 | bytes 12582913 | tf_op jit(solution)/shard_map/jit(_where)/select_n | solution.py:103
  502.6 9.8 %fusion.51 = (bf16[1,1536,1024]{2,0,1:T(2,128)(2,1)S(1)}, bf16[1,1536,1024]{2,0,1:T(2,128)(2,1)}) fusion(bf16[2,1536,1024]{2,0,1:T(2,128)(2,1)S(1)} %broadcast_select_fusion), kind=kLoop, calls=%fused_computation.264 | loop fusion | bytes 12582912 | tf_op jit(solution)/shard_map/slice | solution.py:205
  512.4 8.0 copy_bitcast_fusion
  520.6 6.2 broadcast_in_dim.71
  526.8 88.3 %while.17 = (s32[]{:T(128)}, bf16[384,1024]{1,0:T(8,128)(2,1)S(1)}, bf16[384,1024]{1,0:T(8,128)(2,1)S(1)}, f32[2,1536,1024]{2,1,0:T(8,128)}, bf16[384,1024]{1,0:...) while((s32[]{:T(128)}, bf16[384,1024]{1,0:T(8,128)(2,1)S(1)}, ...), condition=%wide.region_10.11_spmd, body=%wide.region_6.10_spmd.sunk | while | flops 915946752 | bytes 33441472 | solution.py:163
  527.0 1.7 fusion.77
  529.3 2.0 multiply_reduce_fusion.2
  531.4 1.5 fusion.79
  533.2 1.5 fusion.80
  538.0 1.7 fusion.77
  540.3 2.0 multiply_reduce_fusion.2
  542.4 1.5 fusion.79
  544.1 1.5 fusion.80
  545.7 1.4 convolution_bitcast_fusion.4
  549.0 1.7 fusion.77
  551.4 2.0 multiply_reduce_fusion.2
  553.4 1.5 fusion.79
  555.2 1.5 fusion.80
  560.0 1.7 fusion.77
  562.4 2.0 multiply_reduce_fusion.2
  564.4 1.5 fusion.79
  566.2 1.5 fusion.80
  571.0 1.7 fusion.77
  573.4 2.0 multiply_reduce_fusion.2
  575.4 1.5 fusion.79
  577.2 1.5 fusion.80
  582.1 1.7 fusion.77
  584.4 2.0 multiply_reduce_fusion.2
  586.5 1.5 fusion.79
  588.3 1.5 fusion.80
  593.1 1.7 fusion.77
  595.4 2.0 multiply_reduce_fusion.2
  597.5 1.5 fusion.79
  599.2 1.5 fusion.80
  604.0 1.7 fusion.77
  606.4 2.0 multiply_reduce_fusion.2
  608.4 1.5 fusion.79
  610.2 1.5 fusion.80
  615.0 6.1 slice_select_fusion
  621.5 131.2 %collective-permute-done.2 = f32[2,768,1024]{2,1,0:T(8,128)} collective-permute-done((f32[2,768,1024]{2,1,0:T(8,128)S(1)}, f32[2,768,1024]{2,1,0:T(8,128)}, u32[]{:S(2)}, u32[]{:S(2)}) %collective-permute-start.2) | collective-permute-done | bytes 6291488 | tf_op jit(solution)/shard_map/ppermute | solution.py:17
  752.7 12.0 %select_add_fusion = f32[2,768,1024]{2,1,0:T(8,128)} fusion(f32[2,768,1024]{2,1,0:T(8,128)} %collective-permute-done.2, f32[2,1536,1024]{2,1,0:T(8,128)} %get-tuple-element.162, pred[]{:T(512)S(6)} %eq.65), kind=kLoop, calls=%fused_computation.38 | loop fusion | flops 3145728 | bytes 25165824 | tf_op jit(solution)/shard_map/add | solution.py:120
  764.7 3.7 slice_select_fusion.1
  768.5 5.6 collective-permute-done.3
  778.4 7.9 copy.60
  786.3 9.2 %all-to-all-start.1 = ((bf16[64,4,6,1024]{3,1,2,0:T(4,128)(2,1)}), bf16[64,4,6,1024]{3,1,2,0:T(4,128)(2,1)}, u32[]{:S(2)}, u32[]{:S(2)}) async-start(bf16[64,4,6,1024]{3,1,2,0:T(4,128)(2,1)} %copy.60), calls=%async_computation.1 | async-start | bytes 6291456 | tf_op jit(solution)/shard_map/all_to_all | solution.py:93
  795.6 72.7 %all-to-all-done.1 = bf16[64,4,6,1024]{3,1,2,0:T(4,128)(2,1)} async-done(((bf16[64,4,6,1024]{3,1,2,0:T(4,128)(2,1)}), bf16[64,4,6,1024]{3,1,2,0:T(4,128)(2,1)}, u32[]{:S(2)}, u32[]{:S(2)}) %all-to-all-start.1) | async-done | bytes 3145760 | tf_op jit(solution)/shard_map/all_to_all | solution.py:93
  868.3 3.8 gather_fusion.2
  872.2 3.0 fusion.53
  877.2 10.1 %psum.15 = f32[192]{0:T(256)S(1)} all-reduce(f32[192]{0:T(256)S(1)} %fusion.31), channel_id=1, replica_groups=mesh['seq'=64,'head'=4] {'head'}, use_global_device_ids=true, to_apply=%region_12.13 | all-reduce | flops 192 | bytes 1536 | tf_op jit(solution)/shard_map/psum | solution.py:216
  (184 shorter events, 53.7 us)
Async XLA Ops:
  0.6 410.1 %copy-start = (s32[16,96,96]{2,1,0:T(8,128)S(1)}, s32[16,96,96]{2,1,0:T(8,128)}, u32[]{:S(2)}) copy-start(s32[16,96,96]{2,1,0:T(8,128)} %param.13) | copy-start | bytes 1769476
  42.5 87.9 %copy-start.8 = (u32[256]{0:T(256)S(1)}, u32[256]{0:T(256)}, u32[]{:S(2)}) copy-start(u32[256]{0:T(256)} %constant.244) | copy-start | bytes 3076
  42.5 89.1 %copy-start.7 = (s32[192,1]{0,1:T(1,128)S(1)}, s32[192,1]{0,1:T(1,128)}, u32[]{:S(2)}) copy-start(s32[192,1]{0,1:T(1,128)} %param.12) | copy-start | bytes 2308
  126.4 1.7 copy-start.3
  129.8 250.7 %collective-permute-start = (bf16[2,384,1024]{2,0,1:T(2,128)(2,1)S(1)}, bf16[2,384,1024]{2,0,1:T(2,128)(2,1)}, u32[]{:S(2)}, u32[]{:S(2)}) collective-permute-start(bf16[2,384,1024]{2,0,1:T(2,128)(2,1)S(1)} %slice.68), channel_id=1, source_target_pairs={{0,4},{4,0},{8,12},{12,8},{16,20},{20,16},{24,28},{28,24},{32,36},... | collective-permute-start | bytes 4718600 | tf_op jit(solution)/shard_map/ppermute | solution.py:17
  397.1 74.7 %collective-permute-start.1 = (bf16[2,768,1024]{2,0,1:T(2,128)(2,1)}, bf16[2,768,1024]{2,0,1:T(2,128)(2,1)}, u32[]{:S(2)}, u32[]{:S(2)}) collective-permute-start(bf16[2,768,1024]{2,0,1:T(2,128)(2,1)} %broadcast_select_fusion.1), channel_id=1, source_target_pairs={{0,8},{4,12},{8,0},{12,4},{16,24},{20,28},{24,16},{28,20},{32,40},... | collective-permute-start | bytes 9437192 | tf_op jit(solution)/shard_map/ppermute | solution.py:17
  415.8 2.3 copy-start.4
  621.1 131.6 %collective-permute-start.2 = (f32[2,768,1024]{2,1,0:T(8,128)S(1)}, f32[2,768,1024]{2,1,0:T(8,128)}, u32[]{:S(2)}, u32[]{:S(2)}) collective-permute-start(f32[2,768,1024]{2,1,0:T(8,128)S(1)} %slice_select_fusion), channel_id=1, source_target_pairs={{0,8},{4,12},{8,0},{12,4},{16,24},{20,28},{24,16},{28,20},{32,40},... | collective-permute-start | bytes 18874376 | tf_op jit(solution)/shard_map/ppermute | solution.py:17
  764.7 9.4 %copy-start.2 = (f32[2,768,1024]{2,1,0:T(8,128)S(1)}, f32[2,768,1024]{2,1,0:T(8,128)}, u32[]{:S(2)}) copy-start(f32[2,768,1024]{2,1,0:T(8,128)} %select_add_fusion) | copy-start | bytes 18874372
  768.4 5.7 collective-permute-start.3
  786.3 82.0 %all-to-all-start.1 = ((bf16[64,4,6,1024]{3,1,2,0:T(4,128)(2,1)}), bf16[64,4,6,1024]{3,1,2,0:T(4,128)(2,1)}, u32[]{:S(2)}, u32[]{:S(2)}) async-start(bf16[64,4,6,1024]{3,1,2,0:T(4,128)(2,1)} %copy.60), calls=%async_computation.1 | async-start | bytes 6291456 | tf_op jit(solution)/shard_map/all_to_all | solution.py:93
  872.1 4.8 copy-start.5
  872.1 17.2 %copy-start.1 = (s32[16,96,96]{2,1,0:T(8,128)S(1)}, s32[16,96,96]{2,1,0:T(8,128)}, u32[]{:S(2)}) copy-start(s32[16,96,96]{2,1,0:T(8,128)} %param.13) | copy-start | bytes 1769476
  875.2 13.3 %copy-start.6 = (bf16[1,192,1024]{2,0,1:T(2,128)(2,1)S(1)}, bf16[1,192,1024]{2,0,1:T(2,128)(2,1)}, u32[]{:S(2)}) copy-start(bf16[1,192,1024]{2,0,1:T(2,128)(2,1)} %get-tuple-element.244) | copy-start | bytes 1179652
